TPU v7x, 32 devices: a whole 2x2x4 slice. The times are simulated.
32 devices in a mesh: dp: 4 (over z), expert: 8 (over y, x, core).
Axes of the slice: x: 2, y: 2, z: 4, core: 2. Of those that a mesh axis runs over, the one named last changes fastest.
Arguments:
- tokens: bfloat16 [256, 3584], P(('dp', 'expert')), may hold values from -6 to 6
- routes: int32 [256, 8], P(('dp', 'expert')), may hold values from 0 to 63, as said below
- gate_values: bfloat16 [256, 8], P(('dp', 'expert')), may hold values from 0.099609375 to 0.5
- expert_map: int32 [64], replicated, may hold values from 0 to 63, as said below
- row_counts: int32 [32], P(('dp', 'expert')), may hold values from 1 to 8, 224 in all
- gate_weight: bfloat16 [8, 3584, 2048], P('expert', None, 'dp'), may hold values from -0.09375 to 0.09375
- up_weight: bfloat16 [8, 3584, 2048], P('expert', None, 'dp'), may hold values from -0.09375 to 0.09375
- down_weight: bfloat16 [8, 2048, 3584], P('expert', 'dp'), may hold values from -0.125 to 0.125
- delta_in: bfloat16 [8, 8, 3584, 256], P('expert', 'dp'), may hold values from -0.09375 to 0.09375
- delta_out: bfloat16 [8, 8, 256, 3584], P('expert', 'dp'), may hold values from -0.375 to 0.375
Outputs:
- mixed: bfloat16 [256, 3584], P(('dp', 'expert'))
Inputs may be any that keep to these rules, and one draw needn't show every extreme that they name: `routes`: each row names 8 different experts, two in each of 4 different bases; at most 8 rows of one device route to one base, and some device has a base that 8 of its rows route to. `expert_map`: A permutation of the 64 slots.
All inputs are finite; a program needn't handle non-finite values. No bound on the sum of `row_counts` on one device may be relied on, other than what follows from the above.
Results may differ from a plain program's by a relative error of at most 0.015.
Values may be sent and summed in bfloat16 or wider, within the bound.
No kernel may reach another device: no remote copies, remote signals or barrier semaphores. Data moves between devices by JAX's collectives and lax.ppermute only.
A program may use at most 64 MiB of HBM per device.

v0:
```python
import jax
import jax.numpy as jnp
from jax import lax
from jax.sharding import PartitionSpec as P

JSLOT = 8
BTOP = 4


def slot_table(routes, gate_values, expert_map, live_mask):
    experts = expert_map.shape[0]
    identity_ids = jnp.arange(experts, dtype=jnp.int32)
    matches = routes[:, :, None] == identity_ids[None, None, :]
    slot_ids = jnp.sum(jnp.where(matches, expert_map[None, None, :], 0), axis=2)
    chosen = slot_ids[:, :, None] == identity_ids[None, None, :]
    spread = jnp.sum(
        jnp.where(chosen, gate_values.astype(jnp.float32)[:, :, None], jnp.float32(0.0)), axis=1
    )
    spread = jnp.where(live_mask[:, None], spread, jnp.float32(0.0))
    return spread.astype(jnp.bfloat16)


def placement_table(slot_gates, base_count, capacity):
    blocks, row_total, slot_count = slot_gates.shape
    grouped = slot_gates.reshape(blocks, row_total, base_count, slot_count // base_count)
    member = jnp.sum((grouped > 0).astype(jnp.int32), axis=3) > 0
    counted = member.astype(jnp.int32)
    before = jnp.cumsum(counted, axis=1) - counted
    target = jnp.where(member, before, -1)
    return (target[:, :, :, None] == jnp.arange(capacity, dtype=jnp.int32)).astype(jnp.bfloat16)


def slice_term(sent_rows, sent_gates, gate_part, up_part, down_part, in_part, out_part, first_slot):
    slot_span = in_part.shape[0]
    gate_value = jnp.dot(sent_rows, gate_part, preferred_element_type=jnp.float32)
    up_value = jnp.dot(sent_rows, up_part, preferred_element_type=jnp.float32)
    hidden = (jax.nn.silu(gate_value) * up_value).astype(jnp.bfloat16)
    shared = jnp.dot(hidden, down_part, preferred_element_type=jnp.float32)
    gate_total = jnp.sum(sent_gates.astype(jnp.float32), axis=1, keepdims=True)
    own_gates = lax.dynamic_slice_in_dim(sent_gates, first_slot, slot_span, 1).astype(jnp.float32)
    latent = jnp.einsum(
        "nd,jdr->jnr", sent_rows, in_part, preferred_element_type=jnp.float32
    ).astype(jnp.bfloat16)
    lifted = jnp.einsum("jnr,jrd->jnd", latent, out_part, preferred_element_type=jnp.float32)
    deltas = jnp.einsum("nj,jnd->nd", own_gates, lifted)
    return gate_total * shared + deltas


def body(
    tokens,
    routes,
    gate_values,
    expert_map,
    row_counts,
    gate_weight,
    up_weight,
    down_weight,
    delta_in,
    delta_out,
):
    row_total = tokens.shape[0]
    width = tokens.shape[1]
    dp_size = lax.axis_size("dp")
    expert_size = lax.axis_size("expert")
    slot_count = expert_map.shape[0]
    capacity = 2 * BTOP * row_total // expert_size
    live_mask = jnp.arange(row_total, dtype=jnp.int32) < row_counts[0]
    slot_gates = slot_table(routes, gate_values, expert_map, live_mask)
    own_placed = placement_table(slot_gates[None], expert_size, capacity)[0]
    all_tokens, all_gates = (
        lax.all_gather(tokens, "dp", axis=0, tiled=True),
        lax.all_gather(slot_gates, "dp", axis=0, tiled=True),
    )
    placed = placement_table(
        all_gates.reshape(dp_size, row_total, slot_count), expert_size, capacity
    )
    sent_rows = jnp.einsum(
        "nrbc,nrd->nbcd",
        placed,
        all_tokens.reshape(dp_size, row_total, width),
        preferred_element_type=jnp.float32,
    ).astype(jnp.bfloat16)
    sent_gates = jnp.einsum(
        "nrbc,nrbj->nbcj",
        placed,
        all_gates.reshape(dp_size, row_total, expert_size, JSLOT),
        preferred_element_type=jnp.float32,
    ).astype(jnp.bfloat16)
    got_rows, got_gates = (
        lax.all_to_all(sent_rows, "expert", split_axis=1, concat_axis=1, tiled=True),
        lax.all_to_all(sent_gates, "expert", split_axis=1, concat_axis=1, tiled=True),
    )
    flat_rows = got_rows.reshape(-1, width)
    flat_gates = got_gates.reshape(-1, JSLOT)
    slot_span = JSLOT // dp_size
    first_slot = lax.axis_index("dp") * slot_span
    gate_part = gate_weight[0]
    up_part = up_weight[0]
    down_part = down_weight[0]
    in_part = delta_in[0]
    out_part = delta_out[0]
    summed = lax.psum_scatter(
        slice_term(
            flat_rows, flat_gates, gate_part, up_part, down_part, in_part, out_part, first_slot
        ).astype(jnp.bfloat16),
        "dp",
        scatter_dimension=0,
        tiled=True,
    )
    results = lax.all_to_all(
        summed.reshape(expert_size, capacity, width),
        "expert",
        split_axis=0,
        concat_axis=0,
        tiled=True,
    )
    mixed = jnp.einsum("rbc,bcd->rd", own_placed, results, preferred_element_type=jnp.float32)
    return mixed.astype(jnp.bfloat16)


def solution(mesh):
    in_specs = (
        P(("dp", "expert"), None),
        P(("dp", "expert"), None),
        P(("dp", "expert"), None),
        P(),
        P(("dp", "expert")),
        P("expert", None, "dp"),
        P("expert", None, "dp"),
        P("expert", "dp", None),
        P("expert", "dp", None, None),
        P("expert", "dp", None, None),
    )
    out_specs = P(("dp", "expert"), None)
    return jax.shard_map(body, mesh=mesh, in_specs=in_specs, out_specs=out_specs, check_vma=False)
```

profile of v0, /device:TPU:0, one launch (start us, length us, event | category | flops | bytes accessed | tf_op | source)
XLA Modules:
  0.0 162.9 jit_solution(12481493179372716351)
XLA Ops:
  6.5 0.7 convert_element_type.85
  7.9 1.0 select_reduce_fusion.1
  9.0 13.6 %all_gather.6 = bf16[32,64]{1,0:T(8,128)(2,1)S(1)} all-gather(bf16[8,64]{1,0:T(8,128)(2,1)S(1)} %select_convert_fusion.1), channel_id=1, replica_groups=mesh['dp'=4,'expert'=8] {'dp'}, dimensions={0}, use_global_device_ids=true | all-gather | bytes 5120 | tf_op jit(solution)/shard_map/all_gather | solution.py:72
  22.8 0.6 convert_reduce_fusion.1
  23.5 0.2 convolution_convert_fusion.1
  23.7 0.7 reshape.106
  24.4 3.7 %all-to-all-start = ((bf16[8,2,128]{2,1,0:T(2,128)(2,1)}), bf16[8,2,128]{2,1,0:T(2,128)(2,1)S(1)}, u32[]{:S(2)}, u32[]{:S(2)}) async-start(bf16[8,2,128]{2,1,0:T(2,128)(2,1)} %reshape.106), calls=%async_computation | async-start | bytes 8192 | tf_op jit(solution)/shard_map/all_to_all | solution.py:91
  28.1 14.0 %all_gather.7 = bf16[32,3584]{1,0:T(8,128)(2,1)S(1)} all-gather(bf16[8,3584]{1,0:T(8,128)(2,1)} %param.10), channel_id=1, replica_groups=mesh['dp'=4,'expert'=8] {'dp'}, dimensions={0}, use_global_device_ids=true | all-gather | bytes 286720 | tf_op jit(solution)/shard_map/all_gather | solution.py:71
  42.2 0.6 convolution_convert_fusion
  42.8 1.4 copy.45
  44.2 4.3 %all-to-all-start.1 = ((bf16[4,8,8,3584]{3,2,0,1:T(8,128)(2,1)}), bf16[4,8,8,3584]{3,2,0,1:T(8,128)(2,1)}, u32[]{:S(2)}, u32[]{:S(2)}) async-start(bf16[4,8,8,3584]{3,2,0,1:T(8,128)(2,1)} %copy.45), calls=%async_computation.1 | async-start | bytes 3670016 | tf_op jit(solution)/shard_map/all_to_all | solution.py:90
  48.7 0.2 copy.47
  49.0 0.2 copy.49
  49.4 22.9 %all-to-all-done.1 = bf16[4,8,8,3584]{3,2,0,1:T(8,128)(2,1)} async-done(((bf16[4,8,8,3584]{3,2,0,1:T(8,128)(2,1)}), bf16[4,8,8,3584]{3,2,0,1:T(8,128)(2,1)}, u32[]{:S(2)}, u32[]{:S(2)}) %all-to-all-start.1) | async-done | bytes 1835040 | tf_op jit(solution)/shard_map/all_to_all | solution.py:90
  72.3 1.6 %copy.46 = bf16[4,8,8,3584]{3,2,1,0:T(8,128)(2,1)S(1)} copy(bf16[4,8,8,3584]{3,2,0,1:T(8,128)(2,1)} %all-to-all-done.1) | data formatting | bytes 3670016 | tf_op jit(solution)/shard_map/all_to_all | solution.py:90
  74.0 7.1 %fusion.5 = bf16[2,256,3584]{2,1,0:T(8,128)(2,1)} fusion(bf16[1,2,256,3584]{3,2,1,0:T(8,128)(2,1)} %param.19, bf16[256,3584,1]{1,0,2:T(8,128)(2,1)S(1)} %bitcast.66, bf16[1,2,3584,256]{3,2,1,0:T(8,128)(2,1)} %param.18), kind=kOutput, calls=%fused_computation.8 | convolution fusion | flops 1879179264 | bytes 12845056 | tf_op jit(solution)/shard_map/jnr,jrd->jnd/dot_general | solution.py:44
  81.1 14.9 %fusion = f32[256,1,3584]{2,1,0:T(1,128)} fusion(bf16[256,2,1]{1,2,0:T(2,128)(2,1)S(1)} %copy.49, bf16[2,256,3584]{2,1,0:T(8,128)(2,1)} %fusion.5), kind=kOutput, calls=%fused_computation | convolution fusion | flops 3670016 | bytes 7341056 | tf_op jit(solution)/shard_map/nj,jnd->nd/dot_general | solution.py:45
  96.0 1.1 fusion.12
  97.1 7.6 %fusion.3 = bf16[256,3584]{1,0:T(8,128)(2,1)} fusion(bf16[1,512,3584]{2,1,0:T(8,128)(2,1)} %param.17, f32[256,1,3584]{2,1,0:T(1,128)} %fusion, f32[256]{0:T(256)S(1)} %mul.20, bf16[256,3584]{1,0:T(8,128)(2,1)S(1)} %bitcast.68, bf16[1,3584,512]{2,1,0:T(8,128)(2,1)} %param.16, f32[256,512]{1,0:T(8,128)S(1)} %fusion.12), kind=kOutput, calls=%fused_computation.4 | convolution fusion | flops 1882587136 | bytes 15205376 | tf_op jit(solution)/shard_map/dot_general | solution.py:38
  104.8 0.3 convert_reduce_fusion.2
  105.1 37.3 %reduce-scatter.2.cloned.1.call-done = bf16[64,3584]{1,0:T(8,128)(2,1)} async-done(((bf16[256,3584]{1,0:T(8,128)(2,1)}), bf16[64,3584]{1,0:T(8,128)(2,1)}) %reduce-scatter.2.cloned.1.call-update) | async-done | bytes 458768 | tf_op jit(solution)/shard_map/reduce_scatter | solution.py:102
  142.4 3.6 %all-to-all-start.2 = ((bf16[8,8,3584]{2,1,0:T(8,128)(2,1)}), bf16[8,8,3584]{2,1,0:T(8,128)(2,1)S(1)}, u32[]{:S(2)}, u32[]{:S(2)}) async-start(bf16[8,8,3584]{2,1,0:T(8,128)(2,1)} %bitcast.70), calls=%async_computation.3 | async-start | bytes 917504 | tf_op jit(solution)/shard_map/all_to_all | solution.py:110
  146.2 8.9 %all-to-all-done.2 = bf16[8,8,3584]{2,1,0:T(8,128)(2,1)S(1)} async-done(((bf16[8,8,3584]{2,1,0:T(8,128)(2,1)}), bf16[8,8,3584]{2,1,0:T(8,128)(2,1)S(1)}, u32[]{:S(2)}, u32[]{:S(2)}) %all-to-all-start.2) | async-done | bytes 458784 | tf_op jit(solution)/shard_map/all_to_all | solution.py:110
  155.0 1.0 fusion.4
  (25 shorter events, 1.1 us)
Async XLA Ops:
  24.4 19.8 %all-to-all-start = ((bf16[8,2,128]{2,1,0:T(2,128)(2,1)}), bf16[8,2,128]{2,1,0:T(2,128)(2,1)S(1)}, u32[]{:S(2)}, u32[]{:S(2)}) async-start(bf16[8,2,128]{2,1,0:T(2,128)(2,1)} %reshape.106), calls=%async_computation | async-start | bytes 8192 | tf_op jit(solution)/shard_map/all_to_all | solution.py:91
  44.2 28.1 %all-to-all-start.1 = ((bf16[4,8,8,3584]{3,2,0,1:T(8,128)(2,1)}), bf16[4,8,8,3584]{3,2,0,1:T(8,128)(2,1)}, u32[]{:S(2)}, u32[]{:S(2)}) async-start(bf16[4,8,8,3584]{3,2,0,1:T(8,128)(2,1)} %copy.45), calls=%async_computation.1 | async-start | bytes 3670016 | tf_op jit(solution)/shard_map/all_to_all | solution.py:90
  48.5 93.9 %reduce-scatter.2.cloned.1.call-start = ((), (), s32[]{:S(2)}) async-start(), calls=%async_computation.4 | async-start | bytes 2293760 | tf_op jit(solution)/shard_map/reduce_scatter | solution.py:102
  81.1 14.9 %copy-start = (bf16[1,3584,512]{2,1,0:T(8,128)(2,1)S(1)}, bf16[1,3584,512]{2,1,0:T(8,128)(2,1)}, u32[]{:S(2)}) copy-start(bf16[1,3584,512]{2,1,0:T(8,128)(2,1)} %param.15) | copy-start | bytes 11010052
  142.4 12.6 %all-to-all-start.2 = ((bf16[8,8,3584]{2,1,0:T(8,128)(2,1)}), bf16[8,8,3584]{2,1,0:T(8,128)(2,1)S(1)}, u32[]{:S(2)}, u32[]{:S(2)}) async-start(bf16[8,8,3584]{2,1,0:T(8,128)(2,1)} %bitcast.70), calls=%async_computation.3 | async-start | bytes 917504 | tf_op jit(solution)/shard_map/all_to_all | solution.py:110
Sparse Core Ops, SparseCore 0:
  104.9 37.4 reduce-scatter.1
where the time goes:
time: 163 us
  waiting for transfers between devices  69.1 us (42%)
  matrix products  32.6 us (20%)
  blocking collectives  27.7 us (17%)
  between operations  14.2 us (9%)
  starting transfers between devices  11.7 us (7%)
  local copies, waits for them, and re-layouts  4.78 us (3%)
  other arithmetic  2.95 us (2%)
    reduce_scatter x1, waiting for transfers between devices, body(): lax.psum_scatter(slice_term(flat_rows, flat_gates, gate_part, up_part, do...  37.3 us
    all_to_all x1, waiting for transfers between devices, body(): lax.all_to_all(sent_rows, 'expert', split_axis=1, concat_axis=1, tiled=True)  22.9 us
    dot_general x1, matrix products, slice_term(): deltas = jnp.einsum('nj,jnd->nd', own_gates, lifted)  14.9 us
    all_gather x1, blocking collectives, body(): lax.all_gather(tokens, 'dp', axis=0, tiled=True)  14 us
    all_gather x1, blocking collectives, body(): lax.all_gather(slot_gates, 'dp', axis=0, tiled=True)  13.6 us
    all_to_all x1, waiting for transfers between devices, body(): lax.all_to_all(summed.reshape(expert_size, capacity, width), 'expert', sp...  8.9 us
    dot_general x1, matrix products, slice_term(): shared = jnp.dot(hidden, down_part, preferred_element_type=jnp.float32)  7.62 us
    dot_general x1, matrix products, slice_term(): jnp.einsum('jnr,jrd->jnd', latent, out_part, preferred_element_type=jnp.f...  7.14 us
  transfers between devices with their start and end apart: 4, of which 3 were waited for; matrix products, arithmetic and copies ran while one was open for 2% of the time, Pallas kernels for 0%

commit v1 on v0

--- a/solution.py
+++ b/solution.py
@@ -87,7 +87,12 @@
         preferred_element_type=jnp.float32,
     ).astype(jnp.bfloat16)
     got_rows, got_gates = (
-        lax.all_to_all(sent_rows, "expert", split_axis=1, concat_axis=1, tiled=True),
+        jnp.concatenate(
+            lax.all_to_all(
+                jnp.stack(jnp.split(sent_rows, lax.axis_size("expert"), axis=1)), "expert", 0, 0
+            ),
+            axis=1,
+        ),
         lax.all_to_all(sent_gates, "expert", split_axis=1, concat_axis=1, tiled=True),
     )
     flat_rows = got_rows.reshape(-1, width)

time: 163 us -> 164 us (level)
    unnamed x4 -> x15, local copies, waits for them, and re-layouts: 0.83 us -> 3.45 us
  transfers between devices with their start and end apart: 4 -> 4, of which waited for: 3 -> 3; matrix products, arithmetic and copies ran while one was open for 2% -> 1% of each run, Pallas kernels for 0% -> 0%
where the time goes in v1:
time: 164 us
  waiting for transfers between devices  69.1 us (42%)
  matrix products  32.6 us (20%)
  blocking collectives  27.7 us (17%)
  between operations  14.2 us (9%)
  starting transfers between devices  11.5 us (7%)
  local copies, waits for them, and re-layouts  6.02 us (4%)
  other arithmetic  2.95 us (2%)
    reduce_scatter x1, waiting for transfers between devices, body(): lax.psum_scatter(slice_term(flat_rows, flat_gates, gate_part, up_part, do...  37.3 us
    all_to_all x1, waiting for transfers between devices, body(): lax.all_to_all(jnp.stack(jnp.split(sent_rows, lax.axis_size('expert'), ax...  22.9 us
    dot_general x1, matrix products, slice_term(): deltas = jnp.einsum('nj,jnd->nd', own_gates, lifted)  14.9 us
    all_gather x1, blocking collectives, body(): lax.all_gather(tokens, 'dp', axis=0, tiled=True)  14 us
    all_gather x1, blocking collectives, body(): lax.all_gather(slot_gates, 'dp', axis=0, tiled=True)  13.6 us
    all_to_all x1, waiting for transfers between devices, body(): lax.all_to_all(summed.reshape(expert_size, capacity, width), 'expert', sp...  8.9 us
    dot_general x1, matrix products, slice_term(): shared = jnp.dot(hidden, down_part, preferred_element_type=jnp.float32)  7.62 us
    dot_general x1, matrix products, slice_term(): jnp.einsum('jnr,jrd->jnd', latent, out_part, preferred_element_type=jnp.f...  7.14 us
  transfers between devices with their start and end apart: 4, of which 3 were waited for; matrix products, arithmetic and copies ran while one was open for 1% of the time, Pallas kernels for 0%

profile of v1, /device:TPU:0, one launch (start us, length us, event | category | flops | bytes accessed | tf_op | source)
XLA Modules:
  0.0 164.0 jit_solution(5512356673351259789)
XLA Ops:
  6.5 0.7 convert_element_type.85
  7.9 1.0 select_reduce_fusion.1
  9.0 13.6 %all_gather.6 = bf16[32,64]{1,0:T(8,128)(2,1)S(1)} all-gather(bf16[8,64]{1,0:T(8,128)(2,1)S(1)} %select_convert_fusion.1), channel_id=1, replica_groups=mesh['dp'=4,'expert'=8] {'dp'}, dimensions={0}, use_global_device_ids=true | all-gather | bytes 5120 | tf_op jit(solution)/shard_map/all_gather | solution.py:72
  22.8 0.6 convert_reduce_fusion.1
  23.7 0.7 reshape.106
  24.4 3.7 %all-to-all-start = ((bf16[8,2,128]{2,1,0:T(2,128)(2,1)}), bf16[8,2,128]{2,1,0:T(2,128)(2,1)S(1)}, u32[]{:S(2)}, u32[]{:S(2)}) async-start(bf16[8,2,128]{2,1,0:T(2,128)(2,1)} %reshape.106), calls=%async_computation | async-start | bytes 8192 | tf_op jit(solution)/shard_map/all_to_all | solution.py:96
  28.1 14.0 %all_gather.7 = bf16[32,3584]{1,0:T(8,128)(2,1)S(1)} all-gather(bf16[8,3584]{1,0:T(8,128)(2,1)} %param.10), channel_id=1, replica_groups=mesh['dp'=4,'expert'=8] {'dp'}, dimensions={0}, use_global_device_ids=true | all-gather | bytes 286720 | tf_op jit(solution)/shard_map/all_gather | solution.py:71
  42.2 0.6 convolution_convert_fusion
  43.0 1.2 copy-done.1
  44.3 4.0 %all-to-all-start.1 = ((bf16[8,4,1,8,3584]{4,3,1,2,0:T(8,128)(2,1)}), bf16[8,4,1,8,3584]{4,3,1,2,0:T(8,128)(2,1)S(1)}, u32[]{:S(2)}, u32[]{:S(2)}) async-start(bf16[8,4,1,8,3584]{4,3,1,2,0:T(8,128)(2,1)} %copy-done.1), calls=%async_computation.1 | async-start | bytes 3670016 | tf_op jit(solution)/shard_map/all_to_all | solution.py:91
  48.5 0.2 copy.92
  48.8 0.2 copy.94
  49.2 22.9 %all-to-all-done.1 = bf16[8,4,1,8,3584]{4,3,1,2,0:T(8,128)(2,1)S(1)} async-done(((bf16[8,4,1,8,3584]{4,3,1,2,0:T(8,128)(2,1)}), bf16[8,4,1,8,3584]{4,3,1,2,0:T(8,128)(2,1)S(1)}, u32[]{:S(2)}, u32[]{:S(2)}) %all-to-all-start.1) | async-done | bytes 1835040 | tf_op jit(solution)/shard_map/all_to_all | solution.py:91
  72.1 1.3 copy-done
  73.4 1.6 copy.91
  75.0 7.1 %fusion.5 = bf16[2,256,3584]{2,1,0:T(8,128)(2,1)} fusion(bf16[1,2,256,3584]{3,2,1,0:T(8,128)(2,1)} %param.19, bf16[256,3584,1]{1,0,2:T(8,128)(2,1)S(1)} %bitcast.113, bf16[1,2,3584,256]{3,2,1,0:T(8,128)(2,1)} %param.18), kind=kOutput, calls=%fused_computation.8 | convolution fusion | flops 1879179264 | bytes 12845056 | tf_op jit(solution)/shard_map/jnr,jrd->jnd/dot_general | solution.py:44
  82.2 14.9 %fusion = f32[256,1,3584]{2,1,0:T(1,128)} fusion(bf16[256,2,1]{1,2,0:T(2,128)(2,1)S(1)} %copy.94, bf16[2,256,3584]{2,1,0:T(8,128)(2,1)} %fusion.5), kind=kOutput, calls=%fused_computation | convolution fusion | flops 3670016 | bytes 7341056 | tf_op jit(solution)/shard_map/nj,jnd->nd/dot_general | solution.py:45
  97.0 1.1 fusion.12
  98.2 7.6 %fusion.3 = bf16[256,3584]{1,0:T(8,128)(2,1)} fusion(bf16[1,512,3584]{2,1,0:T(8,128)(2,1)} %param.17, f32[256,1,3584]{2,1,0:T(1,128)} %fusion, f32[256]{0:T(256)S(1)} %mul.20, bf16[256,3584]{1,0:T(8,128)(2,1)S(1)} %bitcast.115, bf16[1,3584,512]{2,1,0:T(8,128)(2,1)} %param.16, f32[256,512]{1,0:T(8,128)S(1)} %fusion.12), kind=kOutput, calls=%fused_computation.4 | convolution fusion | flops 1882587136 | bytes 15205376 | tf_op jit(solution)/shard_map/dot_general | solution.py:38
  105.9 0.3 convert_reduce_fusion.2
  106.2 37.3 %reduce-scatter.2.cloned.1.call-done = bf16[64,3584]{1,0:T(8,128)(2,1)} async-done(((bf16[256,3584]{1,0:T(8,128)(2,1)}), bf16[64,3584]{1,0:T(8,128)(2,1)}) %reduce-scatter.2.cloned.1.call-update) | async-done | bytes 458768 | tf_op jit(solution)/shard_map/reduce_scatter | solution.py:107
  143.5 3.7 %all-to-all-start.2 = ((bf16[8,8,3584]{2,1,0:T(8,128)(2,1)}), bf16[8,8,3584]{2,1,0:T(8,128)(2,1)S(1)}, u32[]{:S(2)}, u32[]{:S(2)}) async-start(bf16[8,8,3584]{2,1,0:T(8,128)(2,1)} %bitcast.118), calls=%async_computation.3 | async-start | bytes 917504 | tf_op jit(solution)/shard_map/all_to_all | solution.py:115
  147.3 8.9 %all-to-all-done.2 = bf16[8,8,3584]{2,1,0:T(8,128)(2,1)S(1)} async-done(((bf16[8,8,3584]{2,1,0:T(8,128)(2,1)}), bf16[8,8,3584]{2,1,0:T(8,128)(2,1)S(1)}, u32[]{:S(2)}, u32[]{:S(2)}) %all-to-all-start.2) | async-done | bytes 458784 | tf_op jit(solution)/shard_map/all_to_all | solution.py:115
  156.1 1.0 fusion.4
  (36 shorter events, 1.4 us)
Async XLA Ops:
  24.4 19.8 %all-to-all-start = ((bf16[8,2,128]{2,1,0:T(2,128)(2,1)}), bf16[8,2,128]{2,1,0:T(2,128)(2,1)S(1)}, u32[]{:S(2)}, u32[]{:S(2)}) async-start(bf16[8,2,128]{2,1,0:T(2,128)(2,1)} %reshape.106), calls=%async_computation | async-start | bytes 8192 | tf_op jit(solution)/shard_map/all_to_all | solution.py:96
  43.0 1.3 copy-start.1
  44.3 27.9 %all-to-all-start.1 = ((bf16[8,4,1,8,3584]{4,3,1,2,0:T(8,128)(2,1)}), bf16[8,4,1,8,3584]{4,3,1,2,0:T(8,128)(2,1)S(1)}, u32[]{:S(2)}, u32[]{:S(2)}) async-start(bf16[8,4,1,8,3584]{4,3,1,2,0:T(8,128)(2,1)} %copy-done.1), calls=%async_computation.1 | async-start | bytes 3670016 | tf_op jit(solution)/shard_map/all_to_all | solution.py:91
  48.3 95.2 %reduce-scatter.2.cloned.1.call-start = ((), (), s32[]{:S(2)}) async-start(), calls=%async_computation.4 | async-start | bytes 2293760 | tf_op jit(solution)/shard_map/reduce_scatter | solution.py:107
  72.1 1.3 copy-start
  82.1 14.9 %copy-start.2 = (bf16[1,3584,512]{2,1,0:T(8,128)(2,1)S(1)}, bf16[1,3584,512]{2,1,0:T(8,128)(2,1)}, u32[]{:S(2)}) copy-start(bf16[1,3584,512]{2,1,0:T(8,128)(2,1)} %param.15) | copy-start | bytes 11010052
  143.5 12.7 %all-to-all-start.2 = ((bf16[8,8,3584]{2,1,0:T(8,128)(2,1)}), bf16[8,8,3584]{2,1,0:T(8,128)(2,1)S(1)}, u32[]{:S(2)}, u32[]{:S(2)}) async-start(bf16[8,8,3584]{2,1,0:T(8,128)(2,1)} %bitcast.118), calls=%async_computation.3 | async-start | bytes 917504 | tf_op jit(solution)/shard_map/all_to_all | solution.py:115
Sparse Core Ops, SparseCore 0:
  105.9 37.5 reduce-scatter.1
